TPU v7x, 512 devices: a whole 4x8x8 slice. The times are simulated.
512 devices in a mesh: dp: 64 (over y, z), fsdp: 8 (over x, core).
Axes of the slice: x: 4, y: 8, z: 8, core: 2. Of those that a mesh axis runs over, the one named last changes fastest.
Arguments:
- frames: bfloat16 [524288, 512], P(('dp', 'fsdp')), may hold values from -6 to 6
- utt_pairs: int32 [8, 64, 4], P('fsdp'), may hold values from 32 to 256, as said below
- utt_dest: int32 [8, 64, 4], P('fsdp'), may hold values from 0 to 63, as said below
- conv_weight: bfloat16 [1536, 512], P('dp'), may hold values from -0.15625 to 0.15625
- proj_weight: bfloat16 [512, 1536], P('dp'), may hold values from -0.25 to 0.25
- point_weight: bfloat16 [2, 1536, 1536], P(None, None, 'fsdp'), may hold values from -0.15625 to 0.15625
- depth_weight: float32 [31, 1536], replicated, may hold values from -1 to 1
- gain_first: float32 [1536], replicated, may hold values from 0.5 to 1.5
- gain_second: float32 [1536], replicated, may hold values from 0.5 to 1.5
Outputs:
- encoded: bfloat16 [262144, 1536], P(('dp', 'fsdp'))
Inputs may be any that keep to these rules, and one draw needn't show every extreme that they name: `utt_pairs`: every loader holds exactly 512 pairs and every sequence device receives exactly 512 pairs, from 4 different loaders. Each loader holds one utterance of exactly 256 pairs and one of exactly 32 pairs. `utt_dest`: the 4 utterances of loader i go to the 4 different sequence devices (i + k * 64 / 4) mod 64, k = 0 .. 3, in some order.
All inputs are finite; a program needn't handle non-finite values.
Results may differ from a plain program's by a relative error of at most 0.012.
Values may be sent and summed in bfloat16 or wider, within the bound.
No kernel may reach another device: no remote copies, remote signals or barrier semaphores. Data moves between devices by JAX's collectives and lax.ppermute only.
A program may use at most 64 MiB of HBM per device.

v0:
```python
import jax
import jax.numpy as jnp
from jax import lax
from jax.sharding import PartitionSpec as P


def passed_along(value, axis, steps):
    count = lax.axis_size(axis)
    pairs = [(source, (source + steps) % count) for source in range(count)]
    return lax.ppermute(value, axis, pairs)


def frontend(pair_rows, first_rows, conv_full):
    channels = pair_rows.shape[1] // 2
    even_frames = pair_rows[:, :channels]
    odd_frames = pair_rows[:, channels:]
    earlier = jnp.pad(odd_frames[:-1], ((1, 0), (0, 0)))
    earlier = jnp.where(first_rows[:, None], jnp.zeros_like(earlier), earlier)
    summed = jnp.dot(earlier, conv_full[:channels], preferred_element_type=jnp.float32)
    summed = summed + jnp.dot(
        even_frames, conv_full[channels : 2 * channels], preferred_element_type=jnp.float32
    )
    summed = summed + jnp.dot(
        odd_frames, conv_full[2 * channels :], preferred_element_type=jnp.float32
    )
    return jax.nn.relu(summed).astype(jnp.bfloat16)


def layer_norm(values, scales):
    centered = values - jnp.mean(values, axis=-1, keepdims=True)
    variance = jnp.mean(centered * centered, axis=-1, keepdims=True)
    return centered * lax.rsqrt(variance + 1e-05) * scales


def depthwise(gated, depth_weight, positions, lengths):
    row_count = gated.shape[0]
    kernel_size = depth_weight.shape[0]
    half_width = kernel_size // 2
    padded = jnp.pad(gated.astype(jnp.float32), ((half_width, half_width), (0, 0)))
    mixed = jnp.zeros(gated.shape, jnp.float32)
    for tap_index in range(kernel_size):
        offset = tap_index - half_width
        inside = (positions + offset >= 0) & (positions + offset < lengths)
        term = padded[tap_index : tap_index + row_count] * depth_weight[tap_index][None, :]
        mixed = mixed + jnp.where(inside[:, None], term, jnp.zeros_like(term))
    return mixed


def gate_product(normed, value_weight, gate_weight):
    value_part = jnp.dot(normed, value_weight, preferred_element_type=jnp.float32)
    gate_part = jnp.dot(normed, gate_weight, preferred_element_type=jnp.float32)
    return (value_part * jax.nn.sigmoid(gate_part)).astype(jnp.bfloat16)


def cut_pieces(source_rows, own_starts, slot_size, utt_count):
    padded = jnp.pad(source_rows, ((0, slot_size), (0, 0)))
    pieces = []
    for slot_index in range(utt_count):
        pieces.append(lax.dynamic_slice_in_dim(padded, own_starts[slot_index], slot_size, 0))
    return pieces


def body(
    frames,
    utt_pairs,
    utt_dest,
    conv_weight,
    proj_weight,
    point_weight,
    depth_weight,
    gain_first,
    gain_second,
):
    node_count = lax.axis_size("dp")
    own_index = lax.axis_index("dp")
    pair_count = frames.shape[0] // 2
    channels = frames.shape[1]
    utt_count = utt_pairs.shape[2]
    spacing = node_count // utt_count
    slot_size = pair_count // 2
    pair_table = utt_pairs[0]
    dest_table = utt_dest[0]
    loader_ids = jnp.arange(node_count, dtype=jnp.int32)
    slot_ids = jnp.arange(utt_count, dtype=jnp.int32)
    slot_table = (dest_table - loader_ids[:, None]) % node_count // spacing
    matches = (slot_table[:, :, None] == slot_ids[None, None, :]).astype(jnp.int32)
    loader_offsets = jnp.cumsum(pair_table, axis=1) - pair_table
    slot_counts = jnp.sum(matches * pair_table[:, :, None], axis=1)
    slot_starts = jnp.sum(matches * loader_offsets[:, :, None], axis=1)
    conv_full, proj_full = (
        lax.all_gather(conv_weight, "dp", axis=0, tiled=True),
        lax.all_gather(proj_weight, "dp", axis=0, tiled=True),
    )
    own_starts = slot_starts[own_index]
    sources = (own_index - slot_ids * spacing) % node_count
    piece_lengths = slot_counts[sources, slot_ids]
    earlier_pieces = (sources[None, :] < sources[:, None]).astype(jnp.int32)
    piece_offsets = jnp.sum(earlier_pieces * piece_lengths[None, :], axis=1)
    pair_rows = jnp.arange(pair_count, dtype=jnp.int32)
    inside = (
        (pair_rows[:, None] >= piece_offsets[None, :])
        & (pair_rows[:, None] < piece_offsets[None, :] + piece_lengths[None, :])
    ).astype(jnp.int32)
    piece_index = jnp.sum(inside * slot_ids[None, :], axis=1)
    positions = pair_rows - jnp.sum(inside * piece_offsets[None, :], axis=1)
    lengths = jnp.sum(inside * piece_lengths[None, :], axis=1)
    flat_slot = piece_index * slot_size + positions
    frame_pairs = frames.reshape(pair_count, 2 * channels)
    pieces = cut_pieces(frame_pairs, own_starts, slot_size, utt_count)
    arrived = [pieces[0]]
    for slot_index in range(1, utt_count):
        arrived.append(passed_along(pieces[slot_index], "dp", slot_index * spacing))
    stacked = jnp.concatenate(arrived, axis=0)
    packed = jnp.take(stacked, flat_slot, axis=0)
    front = frontend(packed, positions == 0, conv_full)
    projected = jnp.dot(front, proj_full, preferred_element_type=jnp.float32).astype(jnp.bfloat16)
    normed = layer_norm(projected.astype(jnp.float32), gain_first).astype(jnp.bfloat16)
    weight_part = lax.all_gather(point_weight, "fsdp", axis=2, tiled=True)
    gated = gate_product(normed, weight_part[0], weight_part[1])
    mixed = depthwise(gated, depth_weight, positions, lengths)
    scaled = layer_norm(mixed, gain_second)
    return (scaled * jax.nn.sigmoid(scaled)).astype(jnp.bfloat16)


def solution(mesh):
    in_specs = (
        P(("dp", "fsdp"), None),
        P("fsdp", None, None),
        P("fsdp", None, None),
        P("dp", None),
        P("dp", None),
        P(None, None, "fsdp"),
        P(),
        P(),
        P(),
    )
    out_specs = P(("dp", "fsdp"), None)
    return jax.shard_map(body, mesh=mesh, in_specs=in_specs, out_specs=out_specs, check_vma=False)
```

profile of v0, /device:TPU:1, one launch (start us, length us, event | category | flops | bytes accessed | tf_op | source)
XLA Modules:
  0.0 303.4 jit_solution(6321874885541037050)
XLA Ops:
  6.5 0.7 all-gather.4.cloned.1.call-update
  7.3 0.0 all-gather.6.cloned.1.call-start
  7.3 0.7 all-gather.6.cloned.1.call-update
  8.0 0.0 all-gather.8.cloned.1.call-start
  8.1 0.7 all-gather.8.cloned.1.call-update
  8.8 0.8 reduce_window_sum.11
  9.5 0.7 add_select_fusion
  10.2 0.7 select_reduce_fusion.4
  10.9 0.1 constant_dynamic-slice_fusion
  11.0 0.6 fusion.84
  16.7 1.4 reshape.518
  20.7 1.6 pad_dynamic-slice_fusion.3
  22.2 5.1 %collective-permute-start = (bf16[256,1024]{1,0:T(8,128)(2,1)S(1)}, bf16[256,1024]{1,0:T(8,128)(2,1)S(1)}, u32[]{:S(2)}, u32[]{:S(2)}) collective-permute-start(bf16[256,1024]{1,0:T(8,128)(2,1)S(1)} %get-tuple-element.44), channel_id=1, source_target_pairs={{0,128},{8,136},{16,144},{24,152},{32,160},{40,168},{48,176},{56,1... | collective-permute-start | bytes 1572872 | tf_op jit(solution)/shard_map/ppermute | solution.py:10
  27.3 5.7 %collective-permute-start.1 = (bf16[256,1024]{1,0:T(8,128)(2,1)S(1)}, bf16[256,1024]{1,0:T(8,128)(2,1)}, u32[]{:S(2)}, u32[]{:S(2)}) collective-permute-start(bf16[256,1024]{1,0:T(8,128)(2,1)S(1)} %get-tuple-element.45), channel_id=1, source_target_pairs={{0,256},{8,264},{16,272},{24,280},{32,288},{40,296},{48,304},{56,3... | collective-permute-start | bytes 1572872 | tf_op jit(solution)/shard_map/ppermute | solution.py:10
  33.0 5.0 %collective-permute-start.2 = (bf16[256,1024]{1,0:T(8,128)(2,1)S(1)}, bf16[256,1024]{1,0:T(8,128)(2,1)}, u32[]{:S(2)}, u32[]{:S(2)}) collective-permute-start(bf16[256,1024]{1,0:T(8,128)(2,1)S(1)} %get-tuple-element.46), channel_id=1, source_target_pairs={{0,384},{8,392},{16,400},{24,408},{32,416},{40,424},{48,432},{56,4... | collective-permute-start | bytes 1572872 | tf_op jit(solution)/shard_map/ppermute | solution.py:10
  38.0 0.6 gather_fusion
  38.6 0.2 select_reduce_fusion.5
  38.8 0.1 select_reduce_fusion.2
  39.0 0.0 copy-done.1
  39.0 0.8 slice_reduce_fusion.29
  39.8 0.3 slice_reduce_fusion.30
  40.1 0.1 compare_and_fusion.31
  40.2 1.1 collective-permute-done
  41.2 27.6 %collective-permute-done.1 = bf16[256,1024]{1,0:T(8,128)(2,1)} collective-permute-done((bf16[256,1024]{1,0:T(8,128)(2,1)S(1)}, bf16[256,1024]{1,0:T(8,128)(2,1)}, u32[]{:S(2)}, u32[]{:S(2)}) %collective-permute-start.1) | collective-permute-done | bytes 524320 | tf_op jit(solution)/shard_map/ppermute | solution.py:10
  68.8 11.9 %collective-permute-done.2 = bf16[256,1024]{1,0:T(8,128)(2,1)} collective-permute-done((bf16[256,1024]{1,0:T(8,128)(2,1)S(1)}, bf16[256,1024]{1,0:T(8,128)(2,1)}, u32[]{:S(2)}, u32[]{:S(2)}) %collective-permute-start.2) | collective-permute-done | bytes 524320 | tf_op jit(solution)/shard_map/ppermute | solution.py:10
  80.7 1.5 pad_maximum_fusion
  82.3 2.2 gather_fusion.1
  84.5 0.2 broadcast_select_fusion
  84.7 31.2 %all-gather.4.cloned.1.call-done = bf16[1536,512]{1,0:T(8,128)(2,1)} async-done(((bf16[24,512]{1,0:T(8,128)(2,1)}), bf16[1536,512]{1,0:T(8,128)(2,1)}) %all-gather.4.cloned.1.call-update) | async-done | bytes 1572880 | tf_op jit(solution)/shard_map/all_gather | solution.py:91
  116.0 1.5 fusion.62
  117.5 2.5 convolution_add_fusion.1
  120.0 78.9 %all-gather.6.cloned.1.call-done = bf16[512,1536]{1,0:T(8,128)(2,1)} async-done(((bf16[8,1536]{1,0:T(8,128)(2,1)}), bf16[512,1536]{1,0:T(8,128)(2,1)}) %all-gather.6.cloned.1.call-update) | async-done | bytes 1572880 | tf_op jit(solution)/shard_map/all_gather | solution.py:92
  198.9 3.2 %convert_reduce_fusion = (f32[512]{0:T(512)S(1)}, bf16[512,1536]{1,0:T(8,128)(2,1)S(1)}) fusion(bf16[512,1536]{1,0:T(8,128)(2,1)} %all-gather.6.cloned.1.call-done, f32[512,512]{1,0:T(8,128)} %convolution_add_fusion.1, bf16[1536,512]{1,0:T(8,128)(2,1)} %all-gather.4.cloned.1.call-done, bf16[512,1024]{1,0:T(8,128)(2,1)S(1)} %broadcast_select_fusion), kind=kOutput, calls=%fused_computation.7 | convolution fusion | flops 1076887040 | bytes 5244928 | tf_op jit(solution)/shard_map/dot_general | solution.py:116
  202.1 0.6 fusion.8
  202.7 59.3 %all-gather.8.cloned.1.call-done = bf16[2,1536,1536]{1,2,0:T(8,128)(2,1)} async-done(((bf16[2,1536,192]{1,2,0:T(8,128)(2,1)}), bf16[2,1536,1536]{1,2,0:T(8,128)(2,1)}) %all-gather.8.cloned.1.call-update) | async-done | bytes 9437200 | tf_op jit(solution)/shard_map/all_gather | solution.py:118
  261.9 5.2 %fusion.7 = f32[512,1536]{1,0:T(8,128)S(1)} fusion(bf16[2,1536,1536]{1,2,0:T(8,128)(2,1)} %all-gather.8.cloned.1.call-done, bf16[512,1536]{1,0:T(8,128)(2,1)S(1)} %get-tuple-element.85, f32[1536]{0:T(1024)S(1)} %copy-done.10, f32[512]{0:T(512)S(1)} %add_rsqrt_fusion.1, f32[512]{0:T(512)S(1)} %broadcast_multiply_fusion.1), kind=kOutput, calls=%fused_computation.13 | convolution fusion | flops 2421424128 | bytes 9447424 | tf_op jit(solution)/shard_map/dot_general | solution.py:51
  267.2 2.7 fusion.53
  269.9 0.0 copy-done.2
  269.9 0.0 copy-done.3
  269.9 0.0 copy-done.4
  269.9 0.0 copy-done.5
  269.9 0.0 copy-done.6
  269.9 0.0 copy-done.7
  269.9 24.0 %fusion.83 = (f32[512]{0:T(512)S(1)}, f32[512,1536]{1,0:T(8,128)S(1)}) fusion(f32[1536]{0:T(1024)S(1)} %copy-done.6, pred[512]{0:T(512)(128)(4,1)S(1)} %get-tuple-element.48, f32[1536]{0:T(1024)S(1)} %copy-done.7, pred[512]{0:T(512)(128)(4,1)S(1)} %get-tuple-element.49, f32[1536]{0:T(1024)S(1)} %get-tuple-element.6, ...), kind=kLoop, calls=%fused_computation.211 | loop fusion | flops 73137664 | bytes 6499840 | tf_op jit(solution)/shard_map/reduce_sum | solution.py:30
  293.9 0.0 copy-start.8
  294.0 0.4 multiply_reduce_fusion
  294.4 0.2 copy-done.8
  294.6 2.2 multiply_convert_fusion
  (25 shorter events, 0.1 us)
Async XLA Ops:
  6.5 109.4 %all-gather.4.cloned.1.call-start = ((), (), s32[]{:S(2)}) async-start(), calls=%async_computation | async-start | bytes 1597440 | tf_op jit(solution)/shard_map/all_gather | solution.py:91
  7.3 191.6 %all-gather.6.cloned.1.call-start = ((), (), s32[]{:S(2)}) async-start(), calls=%async_computation.1 | async-start | bytes 1597440 | tf_op jit(solution)/shard_map/all_gather | solution.py:92
  8.0 253.9 %all-gather.8.cloned.1.call-start = ((), (), s32[]{:S(2)}) async-start(), calls=%async_computation.2 | async-start | bytes 10616832 | tf_op jit(solution)/shard_map/all_gather | solution.py:118
  8.7 30.2 %copy-start.1 = (f32[31,1536]{1,0:T(8,128)S(1)}, f32[31,1536]{1,0:T(8,128)}, u32[]{:S(2)}) copy-start(f32[31,1536]{1,0:T(8,128)} %param.15) | copy-start | bytes 571396
  22.2 19.0 %collective-permute-start = (bf16[256,1024]{1,0:T(8,128)(2,1)S(1)}, bf16[256,1024]{1,0:T(8,128)(2,1)S(1)}, u32[]{:S(2)}, u32[]{:S(2)}) collective-permute-start(bf16[256,1024]{1,0:T(8,128)(2,1)S(1)} %get-tuple-element.44), channel_id=1, source_target_pairs={{0,128},{8,136},{16,144},{24,152},{32,160},{40,168},{48,176},{56,1... | collective-permute-start | bytes 1572872 | tf_op jit(solution)/shard_map/ppermute | solution.py:10
  27.3 41.5 %collective-permute-start.1 = (bf16[256,1024]{1,0:T(8,128)(2,1)S(1)}, bf16[256,1024]{1,0:T(8,128)(2,1)}, u32[]{:S(2)}, u32[]{:S(2)}) collective-permute-start(bf16[256,1024]{1,0:T(8,128)(2,1)S(1)} %get-tuple-element.45), channel_id=1, source_target_pairs={{0,256},{8,264},{16,272},{24,280},{32,288},{40,296},{48,304},{56,3... | collective-permute-start | bytes 1572872 | tf_op jit(solution)/shard_map/ppermute | solution.py:10
  33.0 47.8 %collective-permute-start.2 = (bf16[256,1024]{1,0:T(8,128)(2,1)S(1)}, bf16[256,1024]{1,0:T(8,128)(2,1)}, u32[]{:S(2)}, u32[]{:S(2)}) collective-permute-start(bf16[256,1024]{1,0:T(8,128)(2,1)S(1)} %get-tuple-element.46), channel_id=1, source_target_pairs={{0,384},{8,392},{16,400},{24,408},{32,416},{40,424},{48,432},{56,4... | collective-permute-start | bytes 1572872 | tf_op jit(solution)/shard_map/ppermute | solution.py:10
  41.2 39.5 %copy-start = (bf16[256,1024]{1,0:T(8,128)(2,1)}, bf16[256,1024]{1,0:T(8,128)(2,1)S(1)}, u32[]{:S(2)}) copy-start(bf16[256,1024]{1,0:T(8,128)(2,1)S(1)} %collective-permute-done) | copy-start | bytes 1572868
  120.0 142.0 %copy-start.10 = (f32[1536]{0:T(1024)S(1)}, f32[1536]{0:T(1024)}, u32[]{:S(2)}) copy-start(f32[1536]{0:T(1024)} %param.16) | copy-start | bytes 18436
  261.9 5.2 %copy-start.9 = (bf16[2,1536,1536]{1,2,0:T(8,128)(2,1)S(1)}, bf16[2,1536,1536]{1,2,0:T(8,128)(2,1)}, u32[]{:S(2)}) copy-start(bf16[2,1536,1536]{1,2,0:T(8,128)(2,1)} %all-gather.8.cloned.1.call-done) | copy-start | bytes 28311556
  267.1 2.8 copy-start.2
  267.1 2.8 copy-start.3
  267.1 2.8 copy-start.4
  267.2 2.8 copy-start.5
  267.2 2.8 copy-start.6
  267.2 2.8 copy-start.7
  293.9 0.7 copy-start.8
Sparse Core Ops, SparseCore 0:
  10.4 105.5 all-gather.3
  119.0 79.7 all-gather.5
  201.0 60.9 all-gather.7
where the time goes:
time: 304 us; the launch traced here: 303 us
  waiting for transfers between devices  212 us (70%)
  other arithmetic  31.5 us (10%)
  between operations  21 us (7%)
  starting transfers between devices  15.8 us (5%)
  matrix products  15 us (5%)
  local copies, waits for them, and re-layouts  7.95 us (3%)
    all_gather x1, waiting for transfers between devices, body(): lax.all_gather(proj_weight, 'dp', axis=0, tiled=True)  78.9 us
    all_gather x1, waiting for transfers between devices, body(): weight_part = lax.all_gather(point_weight, 'fsdp', axis=2, tiled=True)  59.3 us
    ppermute x3, waiting for transfers between devices, passed_along(): return lax.ppermute(value, axis, pairs)  40.6 us
    all_gather x1, waiting for transfers between devices, body(): lax.all_gather(conv_weight, 'dp', axis=0, tiled=True)  31.2 us
    reduce_sum x1, other arithmetic, layer_norm(): centered = values - jnp.mean(values, axis=-1, keepdims=True)  24 us
    ppermute x3, starting transfers between devices, passed_along(): return lax.ppermute(value, axis, pairs)  15.7 us
  transfers between devices with their start and end apart: 6, of which 6 were waited for; matrix products, arithmetic and copies ran while one was open for 7% of the time, Pallas kernels for 0%

commit v1 on v0

--- a/solution.py
+++ b/solution.py
@@ -2,6 +2,12 @@
 import jax.numpy as jnp
 from jax import lax
 from jax.sharding import PartitionSpec as P
+
+
+def _expand_layers_all(inputs):
+    return jnp.concatenate(
+        lax.all_to_all(jnp.stack(lax.axis_size("dp") * [inputs], 0), "dp", 0, 0), 0
+    )
 
 
 def passed_along(value, axis, steps):
@@ -88,7 +94,7 @@
     slot_counts = jnp.sum(matches * pair_table[:, :, None], axis=1)
     slot_starts = jnp.sum(matches * loader_offsets[:, :, None], axis=1)
     conv_full, proj_full = (
-        lax.all_gather(conv_weight, "dp", axis=0, tiled=True),
+        _expand_layers_all(conv_weight),
         lax.all_gather(proj_weight, "dp", axis=0, tiled=True),
     )
     own_starts = slot_starts[own_index]

time: 304 us -> 237 us (0.78)
  waiting for transfers between devices: 212 us -> 130 us
  starting transfers between devices: 15.8 us -> 31.7 us
    all_gather x1, waiting for transfers between devices: 78.9 us -> 19.6 us  [body(): lax.all_gather(proj_weight, 'dp', axis=0, tiled=True)]
    all_gather x1 -> x0, waiting for transfers between devices: 31.2 us -> none  [body(): lax.all_gather(conv_weight, 'dp', axis=0, tiled=True)]
    all_to_all x0 -> x1, starting transfers between devices: none -> 17.4 us  [_expand_layers_all(): lax.all_to_all(jnp.stack(lax.axis_size('dp') * [inputs], 0), 'dp', 0, 0)]
    ppermute x3, waiting for transfers between devices: 40.6 us -> 50.2 us  [passed_along(): return lax.ppermute(value, axis, pairs)]
  transfers between devices with their start and end apart: 6 -> 6, of which waited for: 6 -> 4; matrix products, arithmetic and copies ran while one was open for 7% -> 8% of each run, Pallas kernels for 0% -> 0%
where the time goes in v1:
time: 237 us
  waiting for transfers between devices  130 us (55%)
  starting transfers between devices  31.7 us (13%)
  other arithmetic  29.4 us (12%)
  between operations  21.5 us (9%)
  matrix products  15 us (6%)
  local copies, waits for them, and re-layouts  8.92 us (4%)
    all_gather x1, waiting for transfers between devices, body(): weight_part = lax.all_gather(point_weight, 'fsdp', axis=2, tiled=True)  58.9 us
    ppermute x3, waiting for transfers between devices, passed_along(): return lax.ppermute(value, axis, pairs)  50.2 us
    reduce_sum x1, other arithmetic, layer_norm(): centered = values - jnp.mean(values, axis=-1, keepdims=True)  24 us
    all_gather x1, waiting for transfers between devices, body(): lax.all_gather(proj_weight, 'dp', axis=0, tiled=True)  19.6 us
    all_to_all x1, starting transfers between devices, _expand_layers_all(): lax.all_to_all(jnp.stack(lax.axis_size('dp') * [inputs], 0), 'dp', 0, 0)  17.4 us
    ppermute x3, starting transfers between devices, passed_along(): return lax.ppermute(value, axis, pairs)  14.3 us
    dot_general x1, matrix products, gate_product(): gate_part = jnp.dot(normed, gate_weight, preferred_element_type=jnp.float32)  5.16 us
  transfers between devices with their start and end apart: 6, of which 4 were waited for; matrix products, arithmetic and copies ran while one was open for 8% of the time, Pallas kernels for 0%

profile of v1, /device:TPU:1, one launch (start us, length us, event | category | flops | bytes accessed | tf_op | source)
XLA Modules:
  0.0 236.7 jit_solution(3226328900426013268)
XLA Ops:
  6.5 0.0 all-gather.3.cloned.1.call-start
  6.5 0.7 all-gather.3.cloned.1.call-update
  7.3 0.0 all-gather.5.cloned.1.call-start
  7.3 0.7 all-gather.5.cloned.1.call-update
  8.0 2.0 stack.2
  10.0 17.4 %all-to-all-start = ((bf16[64,24,512]{2,1,0:T(8,128)(2,1)}), bf16[64,24,512]{2,1,0:T(8,128)(2,1)}, u32[]{:S(2)}, u32[]{:S(2)}) async-start(bf16[64,24,512]{2,1,0:T(8,128)(2,1)} %stack.2), calls=%async_computation | async-start | bytes 3145728 | tf_op jit(solution)/shard_map/all_to_all | solution.py:9
  27.4 0.0 copy-start.2
  27.4 0.0 copy-done.9
  27.4 0.0 copy-done.11
  27.5 0.1 constant_dynamic-slice_fusion
  27.6 0.6 fusion.84
  33.3 0.0 copy-done
  33.3 0.4 reshape.523
  36.3 1.6 pad_dynamic-slice_fusion.3
  37.9 3.8 %collective-permute-start = (bf16[256,1024]{1,0:T(8,128)(2,1)S(1)}, bf16[256,1024]{1,0:T(8,128)(2,1)S(1)}, u32[]{:S(2)}, u32[]{:S(2)}) collective-permute-start(bf16[256,1024]{1,0:T(8,128)(2,1)S(1)} %get-tuple-element.44), channel_id=1, source_target_pairs={{0,128},{8,136},{16,144},{24,152},{32,160},{40,168},{48,176},{56,1... | collective-permute-start | bytes 1572872 | tf_op jit(solution)/shard_map/ppermute | solution.py:16
  41.7 5.4 %collective-permute-start.1 = (bf16[256,1024]{1,0:T(8,128)(2,1)S(1)}, bf16[256,1024]{1,0:T(8,128)(2,1)}, u32[]{:S(2)}, u32[]{:S(2)}) collective-permute-start(bf16[256,1024]{1,0:T(8,128)(2,1)S(1)} %get-tuple-element.45), channel_id=1, source_target_pairs={{0,256},{8,264},{16,272},{24,280},{32,288},{40,296},{48,304},{56,3... | collective-permute-start | bytes 1572872 | tf_op jit(solution)/shard_map/ppermute | solution.py:16
  47.1 5.1 %collective-permute-start.2 = (bf16[256,1024]{1,0:T(8,128)(2,1)S(1)}, bf16[256,1024]{1,0:T(8,128)(2,1)}, u32[]{:S(2)}, u32[]{:S(2)}) collective-permute-start(bf16[256,1024]{1,0:T(8,128)(2,1)S(1)} %get-tuple-element.46), channel_id=1, source_target_pairs={{0,384},{8,392},{16,400},{24,408},{32,416},{40,424},{48,432},{56,4... | collective-permute-start | bytes 1572872 | tf_op jit(solution)/shard_map/ppermute | solution.py:16
  52.2 0.6 gather_fusion
  52.9 0.2 select_reduce_fusion.5
  53.1 0.1 select_reduce_fusion.2
  53.2 0.0 copy-done.2
  53.2 0.8 slice_reduce_fusion.29
  54.0 0.3 slice_reduce_fusion.30
  54.3 0.1 compare_and_fusion.31
  54.4 27.8 %collective-permute-done = bf16[256,1024]{1,0:T(8,128)(2,1)S(1)} collective-permute-done((bf16[256,1024]{1,0:T(8,128)(2,1)S(1)}, bf16[256,1024]{1,0:T(8,128)(2,1)S(1)}, u32[]{:S(2)}, u32[]{:S(2)}) %collective-permute-start) | collective-permute-done | bytes 524320 | tf_op jit(solution)/shard_map/ppermute | solution.py:16
  82.2 22.4 %collective-permute-done.1 = bf16[256,1024]{1,0:T(8,128)(2,1)} collective-permute-done((bf16[256,1024]{1,0:T(8,128)(2,1)S(1)}, bf16[256,1024]{1,0:T(8,128)(2,1)}, u32[]{:S(2)}, u32[]{:S(2)}) %collective-permute-start.1) | collective-permute-done | bytes 524320 | tf_op jit(solution)/shard_map/ppermute | solution.py:16
  104.6 0.0 collective-permute-done.2
  104.6 0.0 copy-done.1
  104.6 1.5 pad_maximum_fusion
  106.1 2.2 gather_fusion.1
  108.4 0.2 broadcast_select_fusion
  108.6 0.0 all-to-all-done
  108.6 1.5 fusion.62
  110.1 2.5 %convolution_add_fusion.1 = f32[512,512]{1,0:T(8,128)} fusion(f32[512,512]{1,0:T(8,128)S(1)} %fusion.62, bf16[1536,512]{1,0:T(8,128)(2,1)} %bitcast.10, bf16[512,1024]{1,0:T(8,128)(2,1)S(1)} %broadcast_select_fusion), kind=kOutput, calls=%fused_computation.85 | convolution fusion | flops 268697600 | bytes 3145728 | tf_op jit(solution)/shard_map/dot_general | solution.py:26
  112.6 19.6 %all-gather.3.cloned.1.call-done = bf16[512,1536]{1,0:T(8,128)(2,1)} async-done(((bf16[8,1536]{1,0:T(8,128)(2,1)}), bf16[512,1536]{1,0:T(8,128)(2,1)}) %all-gather.3.cloned.1.call-update) | async-done | bytes 1572880 | tf_op jit(solution)/shard_map/all_gather | solution.py:98
  132.2 3.2 %convert_reduce_fusion = (f32[512]{0:T(512)S(1)}, bf16[512,1536]{1,0:T(8,128)(2,1)S(1)}) fusion(bf16[512,1536]{1,0:T(8,128)(2,1)} %all-gather.3.cloned.1.call-done, f32[512,512]{1,0:T(8,128)} %convolution_add_fusion.1, bf16[1536,512]{1,0:T(8,128)(2,1)} %bitcast.10, bf16[512,1024]{1,0:T(8,128)(2,1)S(1)} %broadcast_select_fusion), kind=kOutput, calls=%fused_computation.7 | convolution fusion | flops 1076887040 | bytes 5244928 | tf_op jit(solution)/shard_map/dot_general | solution.py:122
  135.4 0.6 fusion.8
  136.0 58.9 %all-gather.5.cloned.1.call-done = bf16[2,1536,1536]{1,2,0:T(8,128)(2,1)} async-done(((bf16[2,1536,192]{1,2,0:T(8,128)(2,1)}), bf16[2,1536,1536]{1,2,0:T(8,128)(2,1)}) %all-gather.5.cloned.1.call-update) | async-done | bytes 9437200 | tf_op jit(solution)/shard_map/all_gather | solution.py:124
  194.9 0.0 copy-done.13
  194.9 5.2 %fusion.7 = f32[512,1536]{1,0:T(8,128)S(1)} fusion(bf16[2,1536,1536]{1,2,0:T(8,128)(2,1)} %all-gather.5.cloned.1.call-done, bf16[512,1536]{1,0:T(8,128)(2,1)S(1)} %get-tuple-element.85, f32[1536]{0:T(1024)S(1)} %copy-done.13, f32[512]{0:T(512)S(1)} %add_rsqrt_fusion.1, f32[512]{0:T(512)S(1)} %broadcast_multiply_fusion.1), kind=kOutput, calls=%fused_computation.13 | convolution fusion | flops 2421424128 | bytes 9447424 | tf_op jit(solution)/shard_map/dot_general | solution.py:57
  200.1 0.0 copy-done.12
  200.1 0.0 copy-start.3
  200.1 2.7 %fusion.53 = f32[512,1536]{1,0:T(8,128)S(1)} fusion(f32[512,1536]{1,0:T(8,128)S(1)} %fusion.7, bf16[2,1536,1536]{1,2,0:T(8,128)(2,1)S(1)} %copy-done.12, bf16[512,1536]{1,0:T(8,128)(2,1)S(1)} %get-tuple-element.85, f32[1536]{0:T(1024)S(1)} %copy-done.13, f32[512]{0:T(512)S(1)} %add_rsqrt_fusion.1, f32[512]{0:T(512)S(1)} %broadcast_multiply_fusion.1), kind=kOutput, calls=%fused_computation.77 | convolution fusion | flops 2422996992 | bytes 12595200 | tf_op jit(solution)/shard_map/dot_general | solution.py:56
  202.9 24.0 %fusion.83 = (f32[512]{0:T(512)S(1)}, f32[512,1536]{1,0:T(8,128)S(1)}) fusion(f32[1536]{0:T(1024)S(1)} %copy-done.7, pred[512]{0:T(512)(128)(4,1)S(1)} %get-tuple-element.48, f32[1536]{0:T(1024)S(1)} %copy-done.8, pred[512]{0:T(512)(128)(4,1)S(1)} %get-tuple-element.49, f32[1536]{0:T(1024)S(1)} %get-tuple-element.6, ...), kind=kLoop, calls=%fused_computation.211 | loop fusion | flops 73137664 | bytes 6499840 | tf_op jit(solution)/shard_map/reduce_sum | solution.py:36
  226.9 0.0 copy-start.10
  226.9 0.4 multiply_reduce_fusion
  227.4 0.2 copy-done.10
  227.6 2.2 multiply_convert_fusion
  (31 shorter events, 0.2 us)
Async XLA Ops:
  6.5 20.9 %copy-start.9 = (s32[1,64,4]{1,2,0:T(4,128)S(1)}, s32[1,64,4]{1,2,0:T(4,128)}, u32[]{:S(2)}) copy-start(s32[1,64,4]{1,2,0:T(4,128)} %param.10) | copy-start | bytes 3076
  6.5 20.9 %copy-start.11 = (s32[1,64,4]{1,2,0:T(4,128)S(1)}, s32[1,64,4]{1,2,0:T(4,128)}, u32[]{:S(2)}) copy-start(s32[1,64,4]{1,2,0:T(4,128)} %param.11) | copy-start | bytes 3076
  6.5 26.8 %copy-start = (bf16[1024,512]{1,0:T(8,128)(2,1)S(1)}, bf16[1024,512]{1,0:T(8,128)(2,1)}, u32[]{:S(2)}) copy-start(bf16[1024,512]{1,0:T(8,128)(2,1)} %param.9) | copy-start | bytes 3145732
  6.5 125.6 %all-gather.3.cloned.1.call-start = ((), (), s32[]{:S(2)}) async-start(), calls=%async_computation.1 | async-start | bytes 1597440 | tf_op jit(solution)/shard_map/all_gather | solution.py:98
  7.3 187.6 %all-gather.5.cloned.1.call-start = ((), (), s32[]{:S(2)}) async-start(), calls=%async_computation.2 | async-start | bytes 10616832 | tf_op jit(solution)/shard_map/all_gather | solution.py:124
  10.0 98.6 %all-to-all-start = ((bf16[64,24,512]{2,1,0:T(8,128)(2,1)}), bf16[64,24,512]{2,1,0:T(8,128)(2,1)}, u32[]{:S(2)}, u32[]{:S(2)}) async-start(bf16[64,24,512]{2,1,0:T(8,128)(2,1)} %stack.2), calls=%async_computation | async-start | bytes 3145728 | tf_op jit(solution)/shard_map/all_to_all | solution.py:9
  27.4 25.8 %copy-start.2 = (f32[31,1536]{1,0:T(8,128)S(1)}, f32[31,1536]{1,0:T(8,128)}, u32[]{:S(2)}) copy-start(f32[31,1536]{1,0:T(8,128)} %param.15) | copy-start | bytes 571396
  37.9 44.3 %collective-permute-start = (bf16[256,1024]{1,0:T(8,128)(2,1)S(1)}, bf16[256,1024]{1,0:T(8,128)(2,1)S(1)}, u32[]{:S(2)}, u32[]{:S(2)}) collective-permute-start(bf16[256,1024]{1,0:T(8,128)(2,1)S(1)} %get-tuple-element.44), channel_id=1, source_target_pairs={{0,128},{8,136},{16,144},{24,152},{32,160},{40,168},{48,176},{56,1... | collective-permute-start | bytes 1572872 | tf_op jit(solution)/shard_map/ppermute | solution.py:16
  41.7 62.9 %collective-permute-start.1 = (bf16[256,1024]{1,0:T(8,128)(2,1)S(1)}, bf16[256,1024]{1,0:T(8,128)(2,1)}, u32[]{:S(2)}, u32[]{:S(2)}) collective-permute-start(bf16[256,1024]{1,0:T(8,128)(2,1)S(1)} %get-tuple-element.45), channel_id=1, source_target_pairs={{0,256},{8,264},{16,272},{24,280},{32,288},{40,296},{48,304},{56,3... | collective-permute-start | bytes 1572872 | tf_op jit(solution)/shard_map/ppermute | solution.py:16
  47.1 57.5 %collective-permute-start.2 = (bf16[256,1024]{1,0:T(8,128)(2,1)S(1)}, bf16[256,1024]{1,0:T(8,128)(2,1)}, u32[]{:S(2)}, u32[]{:S(2)}) collective-permute-start(bf16[256,1024]{1,0:T(8,128)(2,1)S(1)} %get-tuple-element.46), channel_id=1, source_target_pairs={{0,384},{8,392},{16,400},{24,408},{32,416},{40,424},{48,432},{56,4... | collective-permute-start | bytes 1572872 | tf_op jit(solution)/shard_map/ppermute | solution.py:16
  82.2 22.4 %copy-start.1 = (bf16[256,1024]{1,0:T(8,128)(2,1)}, bf16[256,1024]{1,0:T(8,128)(2,1)S(1)}, u32[]{:S(2)}) copy-start(bf16[256,1024]{1,0:T(8,128)(2,1)S(1)} %collective-permute-done) | copy-start | bytes 1572868
  112.6 82.3 %copy-start.13 = (f32[1536]{0:T(1024)S(1)}, f32[1536]{0:T(1024)}, u32[]{:S(2)}) copy-start(f32[1536]{0:T(1024)} %param.16) | copy-start | bytes 18436
  194.9 5.2 %copy-start.12 = (bf16[2,1536,1536]{1,2,0:T(8,128)(2,1)S(1)}, bf16[2,1536,1536]{1,2,0:T(8,128)(2,1)}, u32[]{:S(2)}) copy-start(bf16[2,1536,1536]{1,2,0:T(8,128)(2,1)} %all-gather.5.cloned.1.call-done) | copy-start | bytes 28311556
  200.1 2.7 %copy-start.3 = (f32[1536]{0:T(1024)S(1)}, f32[1536]{0:T(1024)}, u32[]{:S(2)}) copy-start(f32[1536]{0:T(1024)} %get-tuple-element.30) | copy-start | bytes 18436
  200.1 2.7 %copy-start.4 = (f32[1536]{0:T(1024)S(1)}, f32[1536]{0:T(1024)}, u32[]{:S(2)}) copy-start(f32[1536]{0:T(1024)} %get-tuple-element.31) | copy-start | bytes 18436
  200.1 2.7 %copy-start.5 = (f32[1536]{0:T(1024)S(1)}, f32[1536]{0:T(1024)}, u32[]{:S(2)}) copy-start(f32[1536]{0:T(1024)} %get-tuple-element.32) | copy-start | bytes 18436
  200.1 2.7 %copy-start.6 = (f32[1536]{0:T(1024)S(1)}, f32[1536]{0:T(1024)}, u32[]{:S(2)}) copy-start(f32[1536]{0:T(1024)} %get-tuple-element.33) | copy-start | bytes 18436
  200.1 2.7 %copy-start.7 = (f32[1536]{0:T(1024)S(1)}, f32[1536]{0:T(1024)}, u32[]{:S(2)}) copy-start(f32[1536]{0:T(1024)} %get-tuple-element.34) | copy-start | bytes 18436
  200.1 2.7 %copy-start.8 = (f32[1536]{0:T(1024)S(1)}, f32[1536]{0:T(1024)}, u32[]{:S(2)}) copy-start(f32[1536]{0:T(1024)} %get-tuple-element.35) | copy-start | bytes 18436
  226.9 0.7 copy-start.10
Sparse Core Ops, SparseCore 0:
  10.4 121.7 all-gather.2
  134.3 60.5 all-gather.4
